TPU v7x, 512 devices: a whole 4x4x16 slice. The times are simulated.
512 devices in a mesh: segment: 4 (over x), rep: 8 (over y, core), box: 16 (over z).
Axes of the slice: x: 4, y: 4, z: 16, core: 2. Of those that a mesh axis runs over, the one named last changes fastest.
Arguments:
- centers: float32 [512, 4, 4, 512], P(('rep', 'box')), may hold values from -6 to 6
- box_radii: float32 [512, 4, 4, 512], P(('rep', 'box')), may hold values from 0.001 to 0.01
- labels: int32 [512], P(('rep', 'box')), may hold values from 0 to 9
- certified: int32 [512], P(('rep', 'box')), may hold values from 0 to 1, as said below
- conv_weights: bfloat16 [4, 9, 512, 512], P('segment', None, 'box'), may hold values from -0.01171875 to 0.01171875
- conv_bias: float32 [4, 512], P('segment'), may hold values from -1.2 to 1.2
- head_weight: bfloat16 [512, 10], replicated, may hold values from -0.25 to 0.25
- head_bias: float32 [10], replicated, may hold values from -4 to 4
Outputs:
- lower_bounds: float32 [128, 4, 5], P(('rep', 'box'), 'segment')
Inputs may be any that keep to these rules, and one draw needn't show every extreme that they name: `certified`: for each box index and each i, the devices 2i and 2i + 1 along rep hold 4 boxes with value 0 together; in each box index some such pair has all 4 of them on one device.
All inputs are finite; a program needn't handle non-finite values.
Results may differ from a plain program's by a relative error of at most 0.00055.
Values may be sent and summed in bfloat16 or wider, within the bound.
A program may use at most 64 MiB of HBM per device.

v0:
```python
import jax
import jax.numpy as jnp
from jax import lax
from jax.sharding import PartitionSpec as P

K = 5
MICRO = 2
highest = lax.Precision.HIGHEST


def shifted(x, axis, by):
    count = lax.axis_size(axis)
    pairs = [(i, i + by) for i in range(count) if 0 <= i + by < count]
    return lax.ppermute(x, axis, pairs)


def partner(value, axis, apart):
    mask = 2**apart
    pairs = [(source, source ^ mask) for source in range(lax.axis_size(axis))]
    return lax.ppermute(value, axis, pairs)


def in_blocks(x, dim, count):
    lengths = x.shape
    parts = x.reshape(*lengths[:dim], count, lengths[dim] // count, *lengths[dim + 1 :])
    return jnp.moveaxis(parts, dim, 0)


def summed_on_arrival(x, axis, dim):
    count = lax.axis_size(axis)
    parts = lax.all_to_all(in_blocks(x, dim, count), axis, 0, 0, tiled=True)
    return jnp.sum(parts, axis=0)


def convolve(values, kernel_cols):
    extent = values.shape[1]
    padded = jnp.pad(values, ((0, 0), (1, 1), (1, 1), (0, 0)))
    windows = []
    for tap_index in range(9):
        row_shift, col_shift = divmod(tap_index, 3)
        windows.append(padded[:, row_shift : row_shift + extent, col_shift : col_shift + extent, :])
    stacked = jnp.concatenate(windows, axis=3)
    return lax.dot_general(
        stacked, kernel_cols, (((3,), (0,)), ((), ())), preferred_element_type=jnp.float32
    )


def convolve_back(gradient, kernel_rows):
    extent = gradient.shape[1]
    padded = jnp.pad(gradient, ((0, 0), (1, 1), (1, 1), (0, 0)))
    windows = []
    for tap_index in range(9):
        row_shift, col_shift = divmod(tap_index, 3)
        windows.append(
            padded[
                :, 2 - row_shift : 2 - row_shift + extent, 2 - col_shift : 2 - col_shift + extent, :
            ]
        )
    stacked = jnp.concatenate(windows, axis=3)
    return lax.dot_general(
        stacked, kernel_rows, (((3,), (0,)), ((), ())), preferred_element_type=jnp.float32
    )


def forward_layer(middle, radius, kernel_cols, magnitude_cols, shift_bias):
    centre = convolve(middle.astype(jnp.bfloat16), kernel_cols) + shift_bias
    spread = convolve(radius.astype(jnp.bfloat16), magnitude_cols)
    lower_edge = centre - spread
    upper_edge = centre + spread
    upper_pos = jax.nn.relu(upper_edge)
    lower_neg = jax.nn.relu(-lower_edge)
    lower_pos = jax.nn.relu(lower_edge)
    slope_now = upper_pos / (upper_pos + lower_neg)
    intercept = slope_now * lower_neg
    middle = middle + 0.5 * (upper_pos + lower_pos)
    radius = radius + 0.5 * (upper_pos - lower_pos)
    return (middle, radius, slope_now, intercept)


def backward_layer(coeffs, slope_now, intercept, kernel_rows, shift_bias):
    scaled = coeffs * slope_now[:, None]
    layer_term = jnp.sum(
        scaled * shift_bias + jnp.minimum(coeffs, 0.0) * intercept[:, None], axis=(2, 3, 4)
    )
    gradient = scaled.astype(jnp.bfloat16).reshape((-1,) + scaled.shape[2:])
    coeffs = coeffs + convolve_back(gradient, kernel_rows).reshape(coeffs.shape)
    return (coeffs, layer_term)


def head_coeffs(label_box, head_weight, head_bias, extent, channels):
    classes = head_bias.shape[0]
    spec_rows = jnp.arange(K, dtype=jnp.int32)[None, :]
    others = (label_box[:, None] + 1 + spec_rows) % classes
    class_ids = jnp.arange(classes, dtype=jnp.int32)
    selector = (class_ids[None, None, :] == label_box[:, None, None]).astype(jnp.float32) - (
        class_ids[None, None, :] == others[:, :, None]
    ).astype(jnp.float32)
    pooled = jnp.einsum(
        "bkc,fc->bkf", selector, head_weight.astype(jnp.float32), precision=highest
    ) / float(extent * extent)
    offset = jnp.einsum("bkc,c->bk", selector, head_bias, precision=highest)
    coeffs = jnp.broadcast_to(
        pooled[:, :, None, None, :], (label_box.shape[0], K, extent, extent, channels)
    )
    return (coeffs, offset)


def concretize(coeffs, centre_box, radius_box):
    return jnp.sum(
        coeffs * centre_box[:, None] - jnp.abs(coeffs) * radius_box[:, None], axis=(2, 3, 4)
    )


def run_sections(
    centres,
    radii_in,
    labels_in,
    conv_weights,
    conv_bias,
    head_weight,
    head_bias,
    segment_index,
    segment_count,
):
    rows_total = centres.shape[0]
    micro_rows = rows_total // MICRO
    extent = centres.shape[1]
    channels = centres.shape[3]
    kernel = lax.all_gather(conv_weights, "box", axis=2, tiled=True)[0]
    kernel_cols = jnp.transpose(kernel, (0, 2, 1)).reshape(9 * channels, channels)
    magnitude_cols = jnp.abs(kernel_cols)
    shift_bias = conv_bias[0]
    steps_total = MICRO + segment_count - 1
    at_first = segment_index == 0
    at_last = segment_index == segment_count - 1
    block_shape = (micro_rows, extent, extent, channels)
    slopes = jnp.zeros(centres.shape, jnp.float32)
    intercepts = jnp.zeros(centres.shape, jnp.float32)
    incoming = (jnp.zeros(block_shape, jnp.float32), jnp.zeros(block_shape, jnp.float32))

    def section_forward(operands):
        return forward_layer(operands[0], operands[1], kernel_cols, magnitude_cols, shift_bias)

    def spare_forward(operands):
        return (operands[0], operands[1], jnp.zeros_like(operands[0]), jnp.zeros_like(operands[0]))

    for step_index in range(steps_total):
        micro_index = step_index - segment_index
        active = (micro_index >= 0) & (micro_index < MICRO)
        row_start = jnp.clip(micro_index, 0, MICRO - 1) * micro_rows
        own_middle = lax.dynamic_slice_in_dim(centres, row_start, micro_rows, 0)
        own_radius = lax.dynamic_slice_in_dim(radii_in, row_start, micro_rows, 0)
        middle = jnp.where(at_first, own_middle, incoming[0])
        radius = jnp.where(at_first, own_radius, incoming[1])
        new_middle, new_radius, slope_now, intercept = lax.cond(
            active, section_forward, spare_forward, (middle, radius)
        )
        old_slope = lax.dynamic_slice_in_dim(slopes, row_start, micro_rows, 0)
        old_intercept = lax.dynamic_slice_in_dim(intercepts, row_start, micro_rows, 0)
        slopes = lax.dynamic_update_slice_in_dim(
            slopes, jnp.where(active, slope_now, old_slope), row_start, 0
        )
        intercepts = lax.dynamic_update_slice_in_dim(
            intercepts, jnp.where(active, intercept, old_intercept), row_start, 0
        )
        if step_index < steps_total - 1:
            incoming = (
                shifted(new_middle.astype(jnp.bfloat16), "segment", 1).astype(new_middle.dtype),
                shifted(new_radius.astype(jnp.bfloat16), "segment", 1).astype(new_radius.dtype),
            )
    kernel = lax.all_gather(conv_weights, "box", axis=2, tiled=True)[0]
    kernel_rows = kernel.reshape(9 * channels, channels)

    def section_back(operands):
        coeffs, slope_block, intercept_block, centre_block, radius_block, offset = operands
        new_coeffs, layer_term = backward_layer(
            coeffs, slope_block, intercept_block, kernel_rows, shift_bias
        )
        layer_term = layer_term + jnp.where(at_last, offset, 0.0)
        layer_term = layer_term + jnp.where(
            at_first, concretize(new_coeffs, centre_block, radius_block), 0.0
        )
        return (new_coeffs, layer_term)

    def spare_back(operands):
        return (operands[0], jnp.zeros_like(operands[5]))

    contrib = jnp.zeros((rows_total, K), jnp.float32)
    arriving = jnp.zeros((micro_rows, K, extent, extent, channels), jnp.bfloat16)
    for step_index in range(steps_total):
        micro_index = step_index - (segment_count - 1 - segment_index)
        active = (micro_index >= 0) & (micro_index < MICRO)
        row_start = jnp.clip(micro_index, 0, MICRO - 1) * micro_rows
        label_block = lax.dynamic_slice_in_dim(labels_in, row_start, micro_rows, 0)
        head_part, offset = head_coeffs(label_block, head_weight, head_bias, extent, channels)
        coeffs = jnp.where(at_last, head_part, arriving.astype(jnp.float32))
        operands = (
            coeffs,
            lax.dynamic_slice_in_dim(slopes, row_start, micro_rows, 0),
            lax.dynamic_slice_in_dim(intercepts, row_start, micro_rows, 0),
            lax.dynamic_slice_in_dim(centres, row_start, micro_rows, 0),
            lax.dynamic_slice_in_dim(radii_in, row_start, micro_rows, 0),
            offset,
        )
        new_coeffs, layer_term = lax.cond(active, section_back, spare_back, operands)
        old_term = lax.dynamic_slice_in_dim(contrib, row_start, micro_rows, 0)
        contrib = lax.dynamic_update_slice_in_dim(
            contrib, jnp.where(active, layer_term, old_term), row_start, 0
        )
        if step_index < steps_total - 1:
            arriving = shifted(new_coeffs.astype(jnp.bfloat16), "segment", -1)
    return contrib


def per_device(
    centers, box_radii, labels, certified, conv_weights, conv_bias, head_weight, head_bias
):
    segment_count = lax.axis_size("segment")
    segment_index = lax.axis_index("segment")
    box_count = centers.shape[0]
    alive_rows = 1 - certified
    half_rows = box_count // 2
    tail_shape = centers.shape[1:]
    live_rank = jnp.cumsum(alive_rows) - alive_rows
    own_total = jnp.sum(alive_rows)
    slots = jnp.arange(half_rows, dtype=jnp.int32)
    is_live = alive_rows[None, :] > 0
    keep_map = ((slots[:, None] == live_rank[None, :]) & is_live).astype(jnp.float32)
    send_map = ((slots[:, None] + half_rows == live_rank[None, :]) & is_live).astype(jnp.float32)
    fill_map = (slots[:, None] == own_total + slots[None, :]).astype(jnp.float32)
    flat_centres = centers.reshape(box_count, -1)
    flat_radii = box_radii.reshape(box_count, -1)
    label_tags = (labels + 1).astype(jnp.float32)[:, None]
    got_centres, got_radii, got_tags = partner(
        (
            jnp.dot(send_map, flat_centres, precision=highest),
            jnp.dot(send_map, flat_radii, precision=highest),
            jnp.dot(send_map, label_tags, precision=highest),
        ),
        "rep",
        0,
    )
    work_centres = (
        jnp.dot(keep_map, flat_centres, precision=highest)
        + jnp.dot(fill_map, got_centres, precision=highest)
    ).reshape((half_rows,) + tail_shape)
    work_radii = (
        jnp.dot(keep_map, flat_radii, precision=highest)
        + jnp.dot(fill_map, got_radii, precision=highest)
    ).reshape((half_rows,) + tail_shape)
    work_tags = jnp.dot(keep_map, label_tags, precision=highest) + jnp.dot(
        fill_map, got_tags, precision=highest
    )
    work_labels = jnp.maximum(work_tags[:, 0].astype(jnp.int32) - 1, 0)
    contrib = run_sections(
        work_centres,
        work_radii,
        work_labels,
        conv_weights,
        conv_bias,
        head_weight,
        head_bias,
        segment_index,
        segment_count,
    )
    outgoing = jnp.dot(fill_map.T, contrib, precision=highest)
    returned = partner(outgoing, "rep", 0)
    per_box = jnp.dot(keep_map.T, contrib, precision=highest) + jnp.dot(
        send_map.T, returned, precision=highest
    )
    summed = summed_on_arrival(per_box, "segment", 0)
    return summed[None]


def solution(mesh):
    placed = (
        P(("rep", "box"), None, None, None),
        P(("rep", "box"), None, None, None),
        P(("rep", "box")),
        P(("rep", "box")),
        P("segment", None, "box", None),
        P("segment", None),
        P(),
        P(),
    )
    return jax.shard_map(
        per_device,
        mesh=mesh,
        in_specs=placed,
        out_specs=P(("rep", "box"), "segment", None),
        check_vma=False,
    )
```

profile of v0, /device:TPU:1, one launch (start us, length us, event | category | flops | bytes accessed | tf_op | source)
XLA Modules:
  0.0 220.3 jit_solution(12544865204578964342)
XLA Ops:
  6.5 0.7 all-gather.2.cloned.1.call-update
  7.3 1.0 reshape.864
  8.3 0.7 fusion.187
  9.1 0.7 broadcast_compare_fusion
  9.8 1.3 fusion.186
  11.2 0.2 fusion.194
  11.4 8.7 %collective-permute-start.1 = (f32[2,8192]{1,0:T(2,128)S(1)}, f32[2,8192]{1,0:T(2,128)S(1)}, u32[]{:S(2)}, u32[]{:S(2)}) collective-permute-start(f32[2,8192]{1,0:T(2,128)S(1)} %fusion.194), channel_id=1, source_target_pairs={{0,16},{16,0},{32,48},{48,32},{64,80},{80,64},{96,112},{112,96},{1... | collective-permute-start | bytes 196616 | tf_op jit(solution)/shard_map/ppermute | solution.py:20
  20.2 1.0 reshape.866
  21.2 0.2 fusion.196
  21.4 1.9 collective-permute-start.2
  23.5 2.4 %collective-permute-start = (f32[2,1]{0,1:T(1,128)S(1)}, f32[2,1]{0,1:T(1,128)S(1)}, u32[]{:S(2)}, u32[]{:S(2)}) collective-permute-start(f32[2,1]{0,1:T(1,128)S(1)} %convolution_bitcast_fusion.1), channel_id=1, source_target_pairs={{0,16},{16,0},{32,48},{48,32},{64,80},{80,64},{96,112},{112,96},{1... | collective-permute-start | bytes 32 | tf_op jit(solution)/shard_map/ppermute | solution.py:20
  26.0 0.7 iota_add_fusion.1
  26.8 0.3 fusion.193
  27.0 0.2 fusion.195
  27.4 0.7 fusion.188
  31.2 0.6 compare_convert_fusion.4
  31.9 0.7 compare_convert_fusion.3
  32.6 0.5 compare_convert_fusion.2
  33.2 0.6 compare_convert_fusion.1
  33.8 0.7 compare_convert_fusion
  34.9 0.2 convolution_bitcast_fusion.5
  35.1 0.2 convolution_bitcast_fusion.4
  35.3 0.2 convolution_multiply_fusion.2
  36.5 0.3 convolution_add_fusion.1
  36.9 0.2 convolution_add_fusion
  37.2 48.1 %all-gather.2.cloned.1.call-done = bf16[1,9,512,512]{3,2,1,0:T(8,128)(2,1)} async-done(((bf16[1,9,32,512]{3,2,1,0:T(8,128)(2,1)}), bf16[1,9,512,512]{3,2,1,0:T(8,128)(2,1)}) %all-gather.2.cloned.1.call-update) | async-done | bytes 4718608 | tf_op jit(solution)/shard_map/all_gather | solution.py:129
  85.3 6.6 %copy.10 = bf16[9,512,512]{2,1,0:T(8,128)(2,1)} copy(bf16[9,512,512]{1,2,0:T(8,128)(2,1)} %bitcast.356) | data formatting | bytes 9437184 | tf_op jit(solution)/shard_map/transpose | solution.py:130
  92.0 5.1 %bitcast_abs_fusion = bf16[4608,512]{1,0:T(8,128)(2,1)} fusion(bf16[9,512,512]{2,1,0:T(8,128)(2,1)} %copy.10), kind=kLoop, calls=%fused_computation.517 | loop fusion | flops 2359296 | bytes 9437184 | tf_op jit(solution)/shard_map/abs | solution.py:131
  97.1 4.5 %conditional.10 = (f32[1,4,4,512]{3,2,1,0:T(4,128)S(1)}, f32[1,4,4,512]{3,2,1,0:T(4,128)S(1)}, f32[1,4,4,512]{3,2,1,0:T(4,128)S(1)}, f32[1,4,4,512]{3,2,1,0:T(4,128)S(1)}) conditional(s32[]{:T(128)} %convert_element_type.272, (f32[1,4,4,512]{3,2,1,0:T(4,128)S(1)}, f32[1,4,4,512]{3,2,1,0:T(4,128)S(1)}) %tuple.108, (f32[1,4,4,512]{3,2,1,0:T(4,128)S(1)}, ...), branch_computations={%region_2.3_spmd, %region_3.4_spmd} | conditional | flops 151175168 | bytes 10913824 | solution.py:155
  97.3 3.1 %fusion = f32[4,4,512]{2,1,0:T(4,128)S(1)} fusion(bf16[4608,512]{1,0:T(8,128)(2,1)} %get-tuple-element.592, bf16[1,4,4,4608]{3,2,1,0:T(4,128)(2,1)S(1)} %constant_dynamic-update-slice_fusion.9), kind=kOutput, calls=%fused_computation | convolution fusion | flops 75497472 | bytes 4898816 | tf_op jit(solution)/shard_map/cond/branch_1_fun/dot_general | solution.py:43
  100.7 0.8 fusion.4
  101.6 1.3 collective-permute-start.4
  102.9 1.3 collective-permute-start.3
  104.3 0.7 collective-permute-done.3
  105.1 4.9 %conditional.11 = (f32[1,4,4,512]{3,2,1,0:T(4,128)S(1)}, f32[1,4,4,512]{3,2,1,0:T(4,128)S(1)}, f32[1,4,4,512]{3,2,1,0:T(4,128)S(1)}, f32[1,4,4,512]{3,2,1,0:T(4,128)S(1)}) conditional(s32[]{:T(128)} %convert_element_type.273, (f32[1,4,4,512]{3,2,1,0:T(4,128)S(1)}, f32[1,4,4,512]{3,2,1,0:T(4,128)S(1)}) %tuple.110, (f32[1,4,4,512]{3,2,1,0:T(4,128)S(1)}, ...), branch_computations={%region_4.5_spmd, %region_5.6_spmd} | conditional | flops 151175168 | bytes 29788220 | solution.py:155
  105.3 3.3 %fusion.9 = f32[4,4,512]{2,1,0:T(4,128)S(1)} fusion(bf16[4608,512]{1,0:T(8,128)(2,1)} %get-tuple-element.599, bf16[1,4,4,4608]{3,2,1,0:T(4,128)(2,1)S(1)} %constant_dynamic-update-slice_fusion.27), kind=kOutput, calls=%fused_computation.47 | convolution fusion | flops 75497472 | bytes 4898816 | tf_op jit(solution)/shard_map/cond/branch_1_fun/dot_general | solution.py:43
  108.8 0.3 copy-done.2
  109.1 0.8 fusion.13
  110.0 3.6 %collective-permute-start.6 = (bf16[1,4,4,512]{3,2,1,0:T(4,128)(2,1)S(1)}, bf16[1,4,4,512]{3,2,1,0:T(4,128)(2,1)S(1)}, u32[]{:S(2)}, u32[]{:S(2)}) collective-permute-start(bf16[1,4,4,512]{3,2,1,0:T(4,128)(2,1)S(1)} %convert_element_type.281), channel_id=1, source_target_pairs={{0,128},{128,256},{256,384},{1,129},{129,257},{257,385},{2,130},{1... | collective-permute-start | bytes 49160 | tf_op jit(solution)/shard_map/ppermute | solution.py:14
  113.6 1.9 collective-permute-start.5
  115.6 0.8 collective-permute-done.5
  116.5 8.5 %collective-permute-start.8 = (bf16[1,4,4,512]{3,2,1,0:T(4,128)(2,1)S(1)}, bf16[1,4,4,512]{3,2,1,0:T(4,128)(2,1)S(1)}, u32[]{:S(2)}, u32[]{:S(2)}) collective-permute-start(bf16[1,4,4,512]{3,2,1,0:T(4,128)(2,1)S(1)} %convert_element_type.286), channel_id=1, source_target_pairs={{0,128},{128,256},{256,384},{1,129},{129,257},{257,385},{2,130},{1... | collective-permute-start | bytes 49160 | tf_op jit(solution)/shard_map/ppermute | solution.py:14
  125.0 1.9 collective-permute-start.7
  127.0 0.8 collective-permute-done.7
  127.9 3.6 %collective-permute-start.10 = (bf16[1,4,4,512]{3,2,1,0:T(4,128)(2,1)S(1)}, bf16[1,4,4,512]{3,2,1,0:T(4,128)(2,1)S(1)}, u32[]{:S(2)}, u32[]{:S(2)}) collective-permute-start(bf16[1,4,4,512]{3,2,1,0:T(4,128)(2,1)S(1)} %convert_element_type.291), channel_id=1, source_target_pairs={{0,128},{128,256},{256,384},{1,129},{129,257},{257,385},{2,130},{1... | collective-permute-start | bytes 49160 | tf_op jit(solution)/shard_map/ppermute | solution.py:14
  131.5 6.8 %collective-permute-start.9 = (bf16[1,4,4,512]{3,2,1,0:T(4,128)(2,1)S(1)}, bf16[1,4,4,512]{3,2,1,0:T(4,128)(2,1)S(1)}, u32[]{:S(2)}, u32[]{:S(2)}) collective-permute-start(bf16[1,4,4,512]{3,2,1,0:T(4,128)(2,1)S(1)} %convert_element_type.289), channel_id=1, source_target_pairs={{0,128},{128,256},{256,384},{1,129},{129,257},{257,385},{2,130},{1... | collective-permute-start | bytes 49160 | tf_op jit(solution)/shard_map/ppermute | solution.py:14
  138.4 0.8 collective-permute-done.9
  139.5 1.3 collective-permute-start.11
  140.9 4.6 %collective-permute-done.11 = bf16[1,5,4,4,512]{4,1,3,2,0:T(8,128)(2,1)S(1)} collective-permute-done((bf16[1,5,4,4,512]{4,1,3,2,0:T(8,128)(2,1)S(1)}, bf16[1,5,4,4,512]{4,1,3,2,0:T(8,128)(2,1)S(1)}, u32[]{:S(2)}, u32[]{:S(2)}) %collective-permute-start.11) | collective-permute-done | bytes 81952 | tf_op jit(solution)/shard_map/ppermute | solution.py:14
  145.6 1.3 collective-permute-start.12
  146.9 4.6 %collective-permute-done.12 = bf16[1,5,4,4,512]{4,1,3,2,0:T(8,128)(2,1)S(1)} collective-permute-done((bf16[1,5,4,4,512]{4,1,3,2,0:T(8,128)(2,1)S(1)}, bf16[1,5,4,4,512]{4,1,3,2,0:T(8,128)(2,1)S(1)}, u32[]{:S(2)}, u32[]{:S(2)}) %collective-permute-start.12) | collective-permute-done | bytes 81952 | tf_op jit(solution)/shard_map/ppermute | solution.py:14
  151.7 1.3 collective-permute-start.13
  153.0 18.7 %collective-permute-done.13 = bf16[1,5,4,4,512]{4,1,3,2,0:T(8,128)(2,1)S(1)} collective-permute-done((bf16[1,5,4,4,512]{4,1,3,2,0:T(8,128)(2,1)S(1)}, bf16[1,5,4,4,512]{4,1,3,2,0:T(8,128)(2,1)S(1)}, u32[]{:S(2)}, u32[]{:S(2)}) %collective-permute-start.13) | collective-permute-done | bytes 81952 | tf_op jit(solution)/shard_map/ppermute | solution.py:14
  171.7 4.4 %conditional.18 = (f32[1,5,4,4,512]{4,1,3,2,0:T(8,128)S(1)}, f32[1,5]{1,0:T(1,128)S(1)}) conditional(s32[]{:T(128)} %convert_element_type.303, f32[1,5,4,4,512]{4,1,3,2,0:T(8,128)S(1)} %convert_select_fusion, (f32[2,4,4,512]{3,2,1,0:T(4,128)S(1)}, s32[]{:T(128)}, f32[1,5,4,4,512]{4,1,3,2,0:T(8,128)S(1)}, bf16[4608,512]{1,0:T(8,128)(2,1)}, ...), branch_computations={%region_24.25_spmd, %region_25.28_spmd} | conditional | flops 378019872 | bytes 8734866 | solution.py:205
  172.2 3.9 %subtract_reduce_fusion.3 = (f32[5]{0:T(128)S(1)}, f32[1,5,4,4,512]{4,1,3,2,0:T(8,128)S(1)}) fusion(f32[4,4,512]{2,1,0:T(4,128)S(1)} %get-tuple-element.776, f32[4,4,512]{2,1,0:T(4,128)S(1)} %get-tuple-element.777, f32[1,5,4,4,512]{4,1,3,2,0:T(8,128)S(1)} %get-tuple-element.656, bf16[5,4,4,4608]{3,0,2,1:T(8,128)(2,1)S(1)} %fusion.122, ...), kind=kOutput, calls=%fused_computation.349 | convolution fusion | flops 377733120 | bytes 5849108 | tf_op jit(solution)/shard_map/cond/branch_1_fun/dot_general | solution.py:60
  176.2 1.3 collective-permute-start.14
  177.5 4.4 %collective-permute-done.14 = bf16[1,5,4,4,512]{4,1,3,2,0:T(8,128)(2,1)S(1)} collective-permute-done((bf16[1,5,4,4,512]{4,1,3,2,0:T(8,128)(2,1)S(1)}, bf16[1,5,4,4,512]{4,1,3,2,0:T(8,128)(2,1)S(1)}, u32[]{:S(2)}, u32[]{:S(2)}) %collective-permute-start.14) | collective-permute-done | bytes 81952 | tf_op jit(solution)/shard_map/ppermute | solution.py:14
  182.0 4.4 %conditional.19 = (f32[1,5]{1,0:T(1,128)S(1)}) conditional(s32[]{:T(128)} %convert_element_type.308, () %tuple.122, (f32[5,512]{1,0:T(8,128)S(1)}, pred[1,5,4,4,512]{4,1,3,2,0:T(8,128)(4,1)S(1)}, f32[1,5,4,4,512]{4,1,3,2,0:T(8,128)S(1)}, f32[2,4,4,512]{3,2,1,0:T(4,128)S(1)}, s32[]{:T(128)}, /*index=5*/f32[1,512]{1,0:T(1,128)S(1)}, ...), branch_computations={%region_28.29_spmd, %region_29.32_spmd} | conditional | flops 378104352 | bytes 8693898 | solution.py:205
  182.0 0.2 add_reduce_fusion.4
  182.5 3.9 %subtract_reduce_fusion.4 = f32[5]{0:T(128)S(1)} fusion(bf16[5,4,4,4608]{3,0,2,1:T(8,128)(2,1)S(1)} %fusion.144, bf16[4608,512]{1,0:T(8,128)(2,1)} %get-tuple-element.677, f32[4,4,512]{2,1,0:T(4,128)S(1)} %get-tuple-element.782, f32[4,4,512]{2,1,0:T(4,128)S(1)} %get-tuple-element.783, pred[1,5,4,4,512]{4,1,3,2,0:T(8,128)(4,1)S(1)} %get-tuple-element.667, ...), kind=kOutput, calls=%fused_computation.383 | convolution fusion | flops 377774080 | bytes 5736468 | tf_op jit(solution)/shard_map/cond/branch_1_fun/dot_general | solution.py:60
  186.8 18.7 %collective-permute-start.15 = (f32[2,5]{1,0:T(2,128)S(1)}, f32[2,5]{1,0:T(2,128)S(1)}, u32[]{:S(2)}, u32[]{:S(2)}) collective-permute-start(f32[2,5]{1,0:T(2,128)S(1)} %fusion.174), channel_id=1, source_target_pairs={{0,16},{16,0},{32,48},{48,32},{64,80},{80,64},{96,112},{112,96},{1... | collective-permute-start | bytes 128 | tf_op jit(solution)/shard_map/ppermute | solution.py:20
  205.5 0.8 collective-permute-done.15
  206.5 6.5 %all_to_all.5 = f32[4,1,5]{2,1,0:T(1,128)S(1)} all-to-all(f32[4,1,5]{2,1,0:T(1,128)S(1)} %bitcast.376), channel_id=1, replica_groups=mesh['segment'=4,'rep'=8,'box'=16] {'segment'}, dimensions={0} | all-to-all | bytes 160 | tf_op jit(solution)/shard_map/all_to_all | solution.py:31
  212.9 0.5 reduce_sum.109
  (175 shorter events, 5.6 us)
Async XLA Ops:
  6.5 28.8 %copy-start = (bf16[512,10]{0,1:T(8,128)(2,1)S(1)}, bf16[512,10]{0,1:T(8,128)(2,1)}, u32[]{:S(2)}) copy-start(bf16[512,10]{0,1:T(8,128)(2,1)} %param.34) | copy-start | bytes 30724
  6.5 16.8 %copy-start.7 = (s32[4]{0:T(128)S(1)}, s32[4]{0:T(128)}, u32[]{:S(2)}) copy-start(s32[4]{0:T(128)} %param.30) | copy-start | bytes 52
  6.5 27.9 %copy-start.8 = (f32[10]{0:T(128)S(1)}, f32[10]{0:T(128)}, u32[]{:S(2)}) copy-start(f32[10]{0:T(128)} %param.35) | copy-start | bytes 124
  6.5 78.8 %all-gather.2.cloned.1.call-start = ((), (), s32[]{:S(2)}) async-start(), calls=%async_computation.1 | async-start | bytes 5013504 | tf_op jit(solution)/shard_map/all_gather | solution.py:129
  11.4 25.1 %collective-permute-start.1 = (f32[2,8192]{1,0:T(2,128)S(1)}, f32[2,8192]{1,0:T(2,128)S(1)}, u32[]{:S(2)}, u32[]{:S(2)}) collective-permute-start(f32[2,8192]{1,0:T(2,128)S(1)} %fusion.194), channel_id=1, source_target_pairs={{0,16},{16,0},{32,48},{48,32},{64,80},{80,64},{96,112},{112,96},{1... | collective-permute-start | bytes 196616 | tf_op jit(solution)/shard_map/ppermute | solution.py:20
  21.4 15.4 %collective-permute-start.2 = (f32[2,8192]{1,0:T(2,128)S(1)}, f32[2,8192]{1,0:T(2,128)S(1)}, u32[]{:S(2)}, u32[]{:S(2)}) collective-permute-start(f32[2,8192]{1,0:T(2,128)S(1)} %fusion.196), channel_id=1, source_target_pairs={{0,16},{16,0},{32,48},{48,32},{64,80},{80,64},{96,112},{112,96},{1... | collective-permute-start | bytes 196616 | tf_op jit(solution)/shard_map/ppermute | solution.py:20
  23.5 3.8 %collective-permute-start = (f32[2,1]{0,1:T(1,128)S(1)}, f32[2,1]{0,1:T(1,128)S(1)}, u32[]{:S(2)}, u32[]{:S(2)}) collective-permute-start(f32[2,1]{0,1:T(1,128)S(1)} %convolution_bitcast_fusion.1), channel_id=1, source_target_pairs={{0,16},{16,0},{32,48},{48,32},{64,80},{80,64},{96,112},{112,96},{1... | collective-permute-start | bytes 32 | tf_op jit(solution)/shard_map/ppermute | solution.py:20
  92.0 5.1 %copy-start.1 = (bf16[9,512,512]{2,1,0:T(8,128)(2,1)S(1)}, bf16[9,512,512]{2,1,0:T(8,128)(2,1)}, u32[]{:S(2)}) copy-start(bf16[9,512,512]{2,1,0:T(8,128)(2,1)} %copy.10) | copy-start | bytes 14155780
  92.0 5.1 %copy-start.6 = (f32[1,512]{1,0:T(1,128)S(1)}, f32[1,512]{1,0:T(1,128)}, u32[]{:S(2)}) copy-start(f32[1,512]{1,0:T(1,128)} %param.33) | copy-start | bytes 6148
  101.6 2.7 %collective-permute-start.4 = (bf16[1,4,4,512]{3,2,1,0:T(4,128)(2,1)S(1)}, bf16[1,4,4,512]{3,2,1,0:T(4,128)(2,1)S(1)}, u32[]{:S(2)}, u32[]{:S(2)}) collective-permute-start(bf16[1,4,4,512]{3,2,1,0:T(4,128)(2,1)S(1)} %convert_element_type.276), channel_id=1, source_target_pairs={{0,128},{128,256},{256,384},{1,129},{129,257},{257,385},{2,130},{1... | collective-permute-start | bytes 49160 | tf_op jit(solution)/shard_map/ppermute | solution.py:14
  102.9 2.1 collective-permute-start.3
  105.3 3.8 %copy-start.2 = (bf16[4608,512]{1,0:T(8,128)(2,1)S(1)}, bf16[4608,512]{1,0:T(8,128)(2,1)}, u32[]{:S(2)}) copy-start(bf16[4608,512]{1,0:T(8,128)(2,1)} %get-tuple-element.596) | copy-start | bytes 14155780 | tf_op jit(solution)/shard_map/cond
  110.0 5.6 %collective-permute-start.6 = (bf16[1,4,4,512]{3,2,1,0:T(4,128)(2,1)S(1)}, bf16[1,4,4,512]{3,2,1,0:T(4,128)(2,1)S(1)}, u32[]{:S(2)}, u32[]{:S(2)}) collective-permute-start(bf16[1,4,4,512]{3,2,1,0:T(4,128)(2,1)S(1)} %convert_element_type.281), channel_id=1, source_target_pairs={{0,128},{128,256},{256,384},{1,129},{129,257},{257,385},{2,130},{1... | collective-permute-start | bytes 49160 | tf_op jit(solution)/shard_map/ppermute | solution.py:14
  113.6 2.8 %collective-permute-start.5 = (bf16[1,4,4,512]{3,2,1,0:T(4,128)(2,1)S(1)}, bf16[1,4,4,512]{3,2,1,0:T(4,128)(2,1)S(1)}, u32[]{:S(2)}, u32[]{:S(2)}) collective-permute-start(bf16[1,4,4,512]{3,2,1,0:T(4,128)(2,1)S(1)} %convert_element_type.279), channel_id=1, source_target_pairs={{0,128},{128,256},{256,384},{1,129},{129,257},{257,385},{2,130},{1... | collective-permute-start | bytes 49160 | tf_op jit(solution)/shard_map/ppermute | solution.py:14
  116.5 10.5 %collective-permute-start.8 = (bf16[1,4,4,512]{3,2,1,0:T(4,128)(2,1)S(1)}, bf16[1,4,4,512]{3,2,1,0:T(4,128)(2,1)S(1)}, u32[]{:S(2)}, u32[]{:S(2)}) collective-permute-start(bf16[1,4,4,512]{3,2,1,0:T(4,128)(2,1)S(1)} %convert_element_type.286), channel_id=1, source_target_pairs={{0,128},{128,256},{256,384},{1,129},{129,257},{257,385},{2,130},{1... | collective-permute-start | bytes 49160 | tf_op jit(solution)/shard_map/ppermute | solution.py:14
  125.0 2.8 %collective-permute-start.7 = (bf16[1,4,4,512]{3,2,1,0:T(4,128)(2,1)S(1)}, bf16[1,4,4,512]{3,2,1,0:T(4,128)(2,1)S(1)}, u32[]{:S(2)}, u32[]{:S(2)}) collective-permute-start(bf16[1,4,4,512]{3,2,1,0:T(4,128)(2,1)S(1)} %convert_element_type.284), channel_id=1, source_target_pairs={{0,128},{128,256},{256,384},{1,129},{129,257},{257,385},{2,130},{1... | collective-permute-start | bytes 49160 | tf_op jit(solution)/shard_map/ppermute | solution.py:14
  127.9 10.5 %collective-permute-start.10 = (bf16[1,4,4,512]{3,2,1,0:T(4,128)(2,1)S(1)}, bf16[1,4,4,512]{3,2,1,0:T(4,128)(2,1)S(1)}, u32[]{:S(2)}, u32[]{:S(2)}) collective-permute-start(bf16[1,4,4,512]{3,2,1,0:T(4,128)(2,1)S(1)} %convert_element_type.291), channel_id=1, source_target_pairs={{0,128},{128,256},{256,384},{1,129},{129,257},{257,385},{2,130},{1... | collective-permute-start | bytes 49160 | tf_op jit(solution)/shard_map/ppermute | solution.py:14
  131.5 7.6 %collective-permute-start.9 = (bf16[1,4,4,512]{3,2,1,0:T(4,128)(2,1)S(1)}, bf16[1,4,4,512]{3,2,1,0:T(4,128)(2,1)S(1)}, u32[]{:S(2)}, u32[]{:S(2)}) collective-permute-start(bf16[1,4,4,512]{3,2,1,0:T(4,128)(2,1)S(1)} %convert_element_type.289), channel_id=1, source_target_pairs={{0,128},{128,256},{256,384},{1,129},{129,257},{257,385},{2,130},{1... | collective-permute-start | bytes 49160 | tf_op jit(solution)/shard_map/ppermute | solution.py:14
  139.5 6.0 %collective-permute-start.11 = (bf16[1,5,4,4,512]{4,1,3,2,0:T(8,128)(2,1)S(1)}, bf16[1,5,4,4,512]{4,1,3,2,0:T(8,128)(2,1)S(1)}, u32[]{:S(2)}, u32[]{:S(2)}) collective-permute-start(bf16[1,5,4,4,512]{4,1,3,2,0:T(8,128)(2,1)S(1)} %convert_element_type.296), channel_id=1, source_target_pairs={{128,0},{256,128},{384,256},{129,1},{257,129},{385,257},{130,2},{2... | collective-permute-start | bytes 245768 | tf_op jit(solution)/shard_map/ppermute | solution.py:14
  145.6 6.0 %collective-permute-start.12 = (bf16[1,5,4,4,512]{4,1,3,2,0:T(8,128)(2,1)S(1)}, bf16[1,5,4,4,512]{4,1,3,2,0:T(8,128)(2,1)S(1)}, u32[]{:S(2)}, u32[]{:S(2)}) collective-permute-start(bf16[1,5,4,4,512]{4,1,3,2,0:T(8,128)(2,1)S(1)} %convert_element_type.301), channel_id=1, source_target_pairs={{128,0},{256,128},{384,256},{129,1},{257,129},{385,257},{130,2},{2... | collective-permute-start | bytes 245768 | tf_op jit(solution)/shard_map/ppermute | solution.py:14
  151.7 20.0 %collective-permute-start.13 = (bf16[1,5,4,4,512]{4,1,3,2,0:T(8,128)(2,1)S(1)}, bf16[1,5,4,4,512]{4,1,3,2,0:T(8,128)(2,1)S(1)}, u32[]{:S(2)}, u32[]{:S(2)}) collective-permute-start(bf16[1,5,4,4,512]{4,1,3,2,0:T(8,128)(2,1)S(1)} %convert_element_type.306), channel_id=1, source_target_pairs={{128,0},{256,128},{384,256},{129,1},{257,129},{385,257},{130,2},{2... | collective-permute-start | bytes 245768 | tf_op jit(solution)/shard_map/ppermute | solution.py:14
  176.2 5.7 %collective-permute-start.14 = (bf16[1,5,4,4,512]{4,1,3,2,0:T(8,128)(2,1)S(1)}, bf16[1,5,4,4,512]{4,1,3,2,0:T(8,128)(2,1)S(1)}, u32[]{:S(2)}, u32[]{:S(2)}) collective-permute-start(bf16[1,5,4,4,512]{4,1,3,2,0:T(8,128)(2,1)S(1)} %convert_element_type.311), channel_id=1, source_target_pairs={{128,0},{256,128},{384,256},{129,1},{257,129},{385,257},{130,2},{2... | collective-permute-start | bytes 245768 | tf_op jit(solution)/shard_map/ppermute | solution.py:14
  186.8 19.5 %collective-permute-start.15 = (f32[2,5]{1,0:T(2,128)S(1)}, f32[2,5]{1,0:T(2,128)S(1)}, u32[]{:S(2)}, u32[]{:S(2)}) collective-permute-start(f32[2,5]{1,0:T(2,128)S(1)} %fusion.174), channel_id=1, source_target_pairs={{0,16},{16,0},{32,48},{48,32},{64,80},{80,64},{96,112},{112,96},{1... | collective-permute-start | bytes 128 | tf_op jit(solution)/shard_map/ppermute | solution.py:20
Sparse Core Ops, SparseCore 0:
  9.4 75.8 all-gather.1
where the time goes:
time: 221 us; the launch traced here: 220 us
  waiting for transfers between devices  85 us (38%)
  starting transfers between devices  65.8 us (30%)
  matrix products  20.2 us (9%)
  between operations  17.3 us (8%)
  other arithmetic  13.7 us (6%)
  local copies, waits for them, and re-layouts  11.1 us (5%)
  blocking collectives  6.47 us (3%)
    all_gather x1, waiting for transfers between devices, run_sections(): kernel = lax.all_gather(conv_weights, 'box', axis=2, tiled=True)[0]  48.1 us
    ppermute x12, waiting for transfers between devices, shifted(): return lax.ppermute(x, axis, pairs)  35.3 us
    ppermute x12, starting transfers between devices, shifted(): return lax.ppermute(x, axis, pairs)  34.1 us
    ppermute x4, starting transfers between devices, partner(): return lax.ppermute(value, axis, pairs)  31.7 us
    dot_general x4, matrix products, convolve(): lax.dot_general(stacked, kernel_cols, (((3,), (0,)), ((), ())), preferred...  7.97 us
    dot_general x2, matrix products, convolve_back(): lax.dot_general(stacked, kernel_rows, (((3,), (0,)), ((), ())), preferred...  7.83 us
    transpose x1, local copies, waits for them, and re-layouts, run_sections(): jnp.transpose(kernel, (0, 2, 1)).reshape(9 * channels, channels)  6.65 us
    all_to_all x1, blocking collectives, summed_on_arrival(): parts = lax.all_to_all(in_blocks(x, dim, count), axis, 0, 0, tiled=True)  6.47 us
  transfers between devices with their start and end apart: 17, of which 10 were waited for; matrix products, arithmetic and copies ran while one was open for 6% of the time, Pallas kernels for 0%

commit v1 on v0

--- a/solution.py
+++ b/solution.py
@@ -126,7 +126,9 @@
     micro_rows = rows_total // MICRO
     extent = centres.shape[1]
     channels = centres.shape[3]
-    kernel = lax.all_gather(conv_weights, "box", axis=2, tiled=True)[0]
+    kernel = jnp.concatenate(
+        lax.all_to_all(jnp.stack([conv_weights] * lax.axis_size("box")), "box", 0, 0), axis=2
+    )[0]
     kernel_cols = jnp.transpose(kernel, (0, 2, 1)).reshape(9 * channels, channels)
     magnitude_cols = jnp.abs(kernel_cols)
     shift_bias = conv_bias[0]

time: 221 us -> 409 us (1.85)
  waiting for transfers between devices: 85 us -> 262 us
  local copies, waits for them, and re-layouts: 11.1 us -> 18.5 us
  starting transfers between devices: 65.8 us -> 70.4 us
    all_to_all x0 -> x1, waiting for transfers between devices: none -> 225 us  [run_sections(): lax.all_to_all(jnp.stack([conv_weights] * lax.axis_size('box')), 'box', 0...]
    all_gather x1, waiting for transfers between devices: 48.1 us -> 0.02 us  [run_sections(): kernel = lax.all_gather(conv_weights, 'box', axis=2, tiled=True)[0]]
    all_to_all x0 -> x1, starting transfers between devices: none -> 15.9 us  [run_sections(): lax.all_to_all(jnp.stack([conv_weights] * lax.axis_size('box')), 'box', 0...]
    ppermute x4, starting transfers between devices: 31.7 us -> 20.4 us  [partner(): return lax.ppermute(value, axis, pairs)]
    all_to_all x0 -> x1, local copies, waits for them, and re-layouts: none -> 5.33 us  [run_sections(): lax.all_to_all(jnp.stack([conv_weights] * lax.axis_size('box')), 'box', 0...]
  transfers between devices with their start and end apart: 17 -> 18, of which waited for: 10 -> 10; matrix products, arithmetic and copies ran while one was open for 6% -> 9% of each run, Pallas kernels for 0% -> 0%
where the time goes in v1:
time: 409 us; the launch traced here: 408 us
  waiting for transfers between devices  262 us (64%)
  starting transfers between devices  70.4 us (17%)
  matrix products  20.2 us (5%)
  local copies, waits for them, and re-layouts  18.5 us (5%)
  between operations  17.4 us (4%)
  other arithmetic  11.8 us (3%)
  blocking collectives  6.47 us (2%)
    all_to_all x1, waiting for transfers between devices, run_sections(): lax.all_to_all(jnp.stack([conv_weights] * lax.axis_size('box')), 'box', 0...  225 us
    ppermute x12, waiting for transfers between devices, shifted(): return lax.ppermute(x, axis, pairs)  35.8 us
    ppermute x12, starting transfers between devices, shifted(): return lax.ppermute(x, axis, pairs)  34.1 us
    ppermute x4, starting transfers between devices, partner(): return lax.ppermute(value, axis, pairs)  20.4 us
    all_to_all x1, starting transfers between devices, run_sections(): lax.all_to_all(jnp.stack([conv_weights] * lax.axis_size('box')), 'box', 0...  15.9 us
  transfers between devices with their start and end apart: 18, of which 10 were waited for; matrix products, arithmetic and copies ran while one was open for 9% of the time, Pallas kernels for 0%

profile of v1, /device:TPU:1, one launch (start us, length us, event | category | flops | bytes accessed | tf_op | source)
XLA Modules:
  0.0 407.5 jit_solution(8920458082049388918)
XLA Ops:
  6.5 3.8 stack.2
  10.3 15.9 %all-to-all-start = ((bf16[16,1,9,32,512]{4,3,2,1,0:T(8,128)(2,1)}), bf16[16,1,9,32,512]{4,3,2,1,0:T(8,128)(2,1)}, u32[]{:S(2)}, u32[]{:S(2)}) async-start(bf16[16,1,9,32,512]{4,3,2,1,0:T(8,128)(2,1)} %stack.2), calls=%async_computation | async-start | bytes 9437184 | tf_op jit(solution)/shard_map/all_to_all | solution.py:130
  26.3 0.7 all-gather.2.cloned.1.call-update
  27.4 0.6 fusion.186
  28.1 0.2 fusion.194
  28.3 2.9 collective-permute-start.1
  31.3 0.2 fusion.196
  31.6 1.9 collective-permute-start.2
  33.6 2.4 collective-permute-start
  36.2 0.3 fusion.193
  36.4 0.7 iota_add_fusion.1
  37.1 0.2 fusion.195
  37.5 0.7 fusion.188
  41.4 0.6 compare_convert_fusion.4
  42.1 0.6 compare_convert_fusion.3
  42.7 0.7 compare_convert_fusion.2
  43.4 0.6 compare_convert_fusion.1
  44.1 0.7 compare_convert_fusion
  45.1 0.2 convolution_bitcast_fusion.5
  45.6 0.2 convolution_multiply_fusion.2
  46.2 0.2 fusion.148
  46.8 0.3 convolution_add_fusion.1
  47.1 0.2 convolution_add_fusion
  47.5 224.7 %all-to-all-done = bf16[16,1,9,32,512]{4,3,2,1,0:T(8,128)(2,1)} async-done(((bf16[16,1,9,32,512]{4,3,2,1,0:T(8,128)(2,1)}), bf16[16,1,9,32,512]{4,3,2,1,0:T(8,128)(2,1)}, u32[]{:S(2)}, u32[]{:S(2)}) %all-to-all-start) | async-done | bytes 4718624 | tf_op jit(solution)/shard_map/all_to_all | solution.py:130
  272.1 5.3 %copy.11 = bf16[16,1,9,32,512]{4,3,0,2,1:T(8,128)(2,1)} copy(bf16[16,1,9,32,512]{4,3,2,1,0:T(8,128)(2,1)} %all-to-all-done) | data formatting | bytes 9437184 | tf_op jit(solution)/shard_map/all_to_all | solution.py:130
  277.5 6.7 %copy.12 = bf16[9,512,512]{2,1,0:T(8,128)(2,1)} copy(bf16[9,512,512]{1,2,0:T(8,128)(2,1)} %bitcast.364) | data formatting | bytes 9437184 | tf_op jit(solution)/shard_map/transpose | solution.py:132
  284.1 5.1 %bitcast_abs_fusion = bf16[4608,512]{1,0:T(8,128)(2,1)} fusion(bf16[9,512,512]{2,1,0:T(8,128)(2,1)} %copy.12), kind=kLoop, calls=%fused_computation.517 | loop fusion | flops 2359296 | bytes 9437184 | tf_op jit(solution)/shard_map/abs | solution.py:133
  289.3 4.5 %conditional.10 = (f32[1,4,4,512]{3,2,1,0:T(4,128)S(1)}, f32[1,4,4,512]{3,2,1,0:T(4,128)S(1)}, f32[1,4,4,512]{3,2,1,0:T(4,128)S(1)}, f32[1,4,4,512]{3,2,1,0:T(4,128)S(1)}) conditional(s32[]{:T(128)} %convert_element_type.272, (f32[1,4,4,512]{3,2,1,0:T(4,128)S(1)}, f32[1,4,4,512]{3,2,1,0:T(4,128)S(1)}) %tuple.108, (f32[1,4,4,512]{3,2,1,0:T(4,128)S(1)}, ...), branch_computations={%region_2.3_spmd, %region_3.4_spmd} | conditional | flops 151175168 | bytes 10913824 | solution.py:157
  289.5 3.1 fusion
  292.8 0.8 fusion.4
  293.7 1.3 collective-permute-start.4
  295.1 1.3 collective-permute-start.3
  296.5 0.7 collective-permute-done.3
  297.2 4.9 %conditional.11 = (f32[1,4,4,512]{3,2,1,0:T(4,128)S(1)}, f32[1,4,4,512]{3,2,1,0:T(4,128)S(1)}, f32[1,4,4,512]{3,2,1,0:T(4,128)S(1)}, f32[1,4,4,512]{3,2,1,0:T(4,128)S(1)}) conditional(s32[]{:T(128)} %convert_element_type.273, (f32[1,4,4,512]{3,2,1,0:T(4,128)S(1)}, f32[1,4,4,512]{3,2,1,0:T(4,128)S(1)}) %tuple.110, (f32[1,4,4,512]{3,2,1,0:T(4,128)S(1)}, ...), branch_computations={%region_4.5_spmd, %region_5.6_spmd} | conditional | flops 151175168 | bytes 29788220 | solution.py:157
  297.5 3.3 fusion.9
  301.0 0.3 copy-done.2
  301.2 0.8 fusion.13
  302.1 3.6 collective-permute-start.6
  305.8 1.9 collective-permute-start.5
  307.8 0.8 collective-permute-done.5
  308.7 8.5 %collective-permute-start.8 = (bf16[1,4,4,512]{3,2,1,0:T(4,128)(2,1)S(1)}, bf16[1,4,4,512]{3,2,1,0:T(4,128)(2,1)S(1)}, u32[]{:S(2)}, u32[]{:S(2)}) collective-permute-start(bf16[1,4,4,512]{3,2,1,0:T(4,128)(2,1)S(1)} %convert_element_type.286), channel_id=1, source_target_pairs={{0,128},{128,256},{256,384},{1,129},{129,257},{257,385},{2,130},{1... | collective-permute-start | bytes 49160 | tf_op jit(solution)/shard_map/ppermute | solution.py:14
  317.2 1.9 collective-permute-start.7
  319.2 0.8 collective-permute-done.7
  320.0 0.2 conditional.13
  320.2 3.6 collective-permute-start.10
  323.9 6.8 %collective-permute-start.9 = (bf16[1,4,4,512]{3,2,1,0:T(4,128)(2,1)S(1)}, bf16[1,4,4,512]{3,2,1,0:T(4,128)(2,1)S(1)}, u32[]{:S(2)}, u32[]{:S(2)}) collective-permute-start(bf16[1,4,4,512]{3,2,1,0:T(4,128)(2,1)S(1)} %convert_element_type.289), channel_id=1, source_target_pairs={{0,128},{128,256},{256,384},{1,129},{129,257},{257,385},{2,130},{1... | collective-permute-start | bytes 49160 | tf_op jit(solution)/shard_map/ppermute | solution.py:14
  330.7 0.8 collective-permute-done.9
  331.7 1.3 collective-permute-start.11
  333.1 4.6 %collective-permute-done.11 = bf16[1,5,4,4,512]{4,1,3,2,0:T(8,128)(2,1)S(1)} collective-permute-done((bf16[1,5,4,4,512]{4,1,3,2,0:T(8,128)(2,1)S(1)}, bf16[1,5,4,4,512]{4,1,3,2,0:T(8,128)(2,1)S(1)}, u32[]{:S(2)}, u32[]{:S(2)}) %collective-permute-start.11) | collective-permute-done | bytes 81952 | tf_op jit(solution)/shard_map/ppermute | solution.py:14
  337.8 1.3 collective-permute-start.12
  339.1 4.4 %collective-permute-done.12 = bf16[1,5,4,4,512]{4,1,3,2,0:T(8,128)(2,1)S(1)} collective-permute-done((bf16[1,5,4,4,512]{4,1,3,2,0:T(8,128)(2,1)S(1)}, bf16[1,5,4,4,512]{4,1,3,2,0:T(8,128)(2,1)S(1)}, u32[]{:S(2)}, u32[]{:S(2)}) %collective-permute-start.12) | collective-permute-done | bytes 81952 | tf_op jit(solution)/shard_map/ppermute | solution.py:14
  343.6 1.3 collective-permute-start.13
  344.9 19.0 %collective-permute-done.13 = bf16[1,5,4,4,512]{4,1,3,2,0:T(8,128)(2,1)S(1)} collective-permute-done((bf16[1,5,4,4,512]{4,1,3,2,0:T(8,128)(2,1)S(1)}, bf16[1,5,4,4,512]{4,1,3,2,0:T(8,128)(2,1)S(1)}, u32[]{:S(2)}, u32[]{:S(2)}) %collective-permute-start.13) | collective-permute-done | bytes 81952 | tf_op jit(solution)/shard_map/ppermute | solution.py:14
  364.0 4.4 %conditional.18 = (f32[1,5,4,4,512]{4,1,3,2,0:T(8,128)S(1)}, f32[1,5]{1,0:T(1,128)S(1)}) conditional(s32[]{:T(128)} %convert_element_type.303, f32[1,5,4,4,512]{4,1,3,2,0:T(8,128)S(1)} %convert_select_fusion, (f32[2,4,4,512]{3,2,1,0:T(4,128)S(1)}, s32[]{:T(128)}, f32[1,5,4,4,512]{4,1,3,2,0:T(8,128)S(1)}, bf16[4608,512]{1,0:T(8,128)(2,1)}, ...), branch_computations={%region_24.25_spmd, %region_25.28_spmd} | conditional | flops 378019872 | bytes 8734866 | solution.py:207
  364.5 3.9 subtract_reduce_fusion.3
  368.5 1.3 collective-permute-start.14
  369.8 4.7 %collective-permute-done.14 = bf16[1,5,4,4,512]{4,1,3,2,0:T(8,128)(2,1)S(1)} collective-permute-done((bf16[1,5,4,4,512]{4,1,3,2,0:T(8,128)(2,1)S(1)}, bf16[1,5,4,4,512]{4,1,3,2,0:T(8,128)(2,1)S(1)}, u32[]{:S(2)}, u32[]{:S(2)}) %collective-permute-start.14) | collective-permute-done | bytes 81952 | tf_op jit(solution)/shard_map/ppermute | solution.py:14
  374.6 4.4 %conditional.19 = (f32[1,5]{1,0:T(1,128)S(1)}) conditional(s32[]{:T(128)} %convert_element_type.308, () %tuple.122, (f32[5,512]{1,0:T(8,128)S(1)}, pred[1,5,4,4,512]{4,1,3,2,0:T(8,128)(4,1)S(1)}, f32[1,5,4,4,512]{4,1,3,2,0:T(8,128)S(1)}, f32[2,4,4,512]{3,2,1,0:T(4,128)S(1)}, s32[]{:T(128)}, /*index=5*/f32[1,512]{1,0:T(1,128)S(1)}, ...), branch_computations={%region_28.29_spmd, %region_29.32_spmd} | conditional | flops 378104352 | bytes 8693898 | solution.py:207
  374.7 0.2 add_reduce_fusion.4
  375.1 3.9 subtract_reduce_fusion.4
  379.5 13.2 %collective-permute-start.15 = (f32[2,5]{1,0:T(2,128)S(1)}, f32[2,5]{1,0:T(2,128)S(1)}, u32[]{:S(2)}, u32[]{:S(2)}) collective-permute-start(f32[2,5]{1,0:T(2,128)S(1)} %fusion.174), channel_id=1, source_target_pairs={{0,16},{16,0},{32,48},{48,32},{64,80},{80,64},{96,112},{112,96},{1... | collective-permute-start | bytes 128 | tf_op jit(solution)/shard_map/ppermute | solution.py:20
  392.7 0.8 collective-permute-done.15
  393.7 6.5 %all_to_all.10 = f32[4,1,5]{2,1,0:T(1,128)S(1)} all-to-all(f32[4,1,5]{2,1,0:T(1,128)S(1)} %bitcast.380), channel_id=1, replica_groups=mesh['segment'=4,'rep'=8,'box'=16] {'segment'}, dimensions={0} | all-to-all | bytes 160 | tf_op jit(solution)/shard_map/all_to_all | solution.py:31
  400.1 0.5 reduce_sum.109
  (185 shorter events, 5.7 us)
Async XLA Ops:
  6.5 39.0 %copy-start = (bf16[512,10]{0,1:T(8,128)(2,1)S(1)}, bf16[512,10]{0,1:T(8,128)(2,1)}, u32[]{:S(2)}) copy-start(bf16[512,10]{0,1:T(8,128)(2,1)} %param.34) | copy-start | bytes 30724
  10.3 16.7 %copy-start.7 = (f32[4,4,4,512]{3,2,1,0:T(4,128)S(1)}, f32[4,4,4,512]{3,2,1,0:T(4,128)}, u32[]{:S(2)}) copy-start(f32[4,4,4,512]{3,2,1,0:T(4,128)} %param.28) | copy-start | bytes 393220
  10.3 16.8 %copy-start.9 = (s32[4]{0:T(128)S(1)}, s32[4]{0:T(128)}, u32[]{:S(2)}) copy-start(s32[4]{0:T(128)} %param.31) | copy-start | bytes 52
  10.3 20.9 %copy-start.8 = (f32[4,4,4,512]{3,2,1,0:T(4,128)S(1)}, f32[4,4,4,512]{3,2,1,0:T(4,128)}, u32[]{:S(2)}) copy-start(f32[4,4,4,512]{3,2,1,0:T(4,128)} %param.29) | copy-start | bytes 393220
  10.3 261.8 %all-to-all-start = ((bf16[16,1,9,32,512]{4,3,2,1,0:T(8,128)(2,1)}), bf16[16,1,9,32,512]{4,3,2,1,0:T(8,128)(2,1)}, u32[]{:S(2)}, u32[]{:S(2)}) async-start(bf16[16,1,9,32,512]{4,3,2,1,0:T(8,128)(2,1)} %stack.2), calls=%async_computation | async-start | bytes 9437184 | tf_op jit(solution)/shard_map/all_to_all | solution.py:130
  26.3 7.2 %copy-start.10 = (s32[4]{0:T(128)S(1)}, s32[4]{0:T(128)}, u32[]{:S(2)}) copy-start(s32[4]{0:T(128)} %param.30) | copy-start | bytes 52
  26.3 18.5 %copy-start.11 = (f32[10]{0:T(128)S(1)}, f32[10]{0:T(128)}, u32[]{:S(2)}) copy-start(f32[10]{0:T(128)} %param.35) | copy-start | bytes 124
  26.3 305.3 %all-gather.2.cloned.1.call-start = ((), (), s32[]{:S(2)}) async-start(), calls=%async_computation.2 | async-start | bytes 5013504 | tf_op jit(solution)/shard_map/all_gather | solution.py:173
  28.3 18.4 %collective-permute-start.1 = (f32[2,8192]{1,0:T(2,128)S(1)}, f32[2,8192]{1,0:T(2,128)S(1)}, u32[]{:S(2)}, u32[]{:S(2)}) collective-permute-start(f32[2,8192]{1,0:T(2,128)S(1)} %fusion.194), channel_id=1, source_target_pairs={{0,16},{16,0},{32,48},{48,32},{64,80},{80,64},{96,112},{112,96},{1... | collective-permute-start | bytes 196616 | tf_op jit(solution)/shard_map/ppermute | solution.py:20
  31.6 15.5 %collective-permute-start.2 = (f32[2,8192]{1,0:T(2,128)S(1)}, f32[2,8192]{1,0:T(2,128)S(1)}, u32[]{:S(2)}, u32[]{:S(2)}) collective-permute-start(f32[2,8192]{1,0:T(2,128)S(1)} %fusion.196), channel_id=1, source_target_pairs={{0,16},{16,0},{32,48},{48,32},{64,80},{80,64},{96,112},{112,96},{1... | collective-permute-start | bytes 196616 | tf_op jit(solution)/shard_map/ppermute | solution.py:20
  33.6 3.8 collective-permute-start
  284.1 5.1 %copy-start.1 = (bf16[9,512,512]{2,1,0:T(8,128)(2,1)S(1)}, bf16[9,512,512]{2,1,0:T(8,128)(2,1)}, u32[]{:S(2)}) copy-start(bf16[9,512,512]{2,1,0:T(8,128)(2,1)} %copy.12) | copy-start | bytes 14155780
  284.1 5.1 %copy-start.6 = (f32[1,512]{1,0:T(1,128)S(1)}, f32[1,512]{1,0:T(1,128)}, u32[]{:S(2)}) copy-start(f32[1,512]{1,0:T(1,128)} %param.33) | copy-start | bytes 6148
  293.7 2.7 collective-permute-start.4
  295.1 2.1 collective-permute-start.3
  297.5 3.8 copy-start.2
  302.1 5.6 %collective-permute-start.6 = (bf16[1,4,4,512]{3,2,1,0:T(4,128)(2,1)S(1)}, bf16[1,4,4,512]{3,2,1,0:T(4,128)(2,1)S(1)}, u32[]{:S(2)}, u32[]{:S(2)}) collective-permute-start(bf16[1,4,4,512]{3,2,1,0:T(4,128)(2,1)S(1)} %convert_element_type.281), channel_id=1, source_target_pairs={{0,128},{128,256},{256,384},{1,129},{129,257},{257,385},{2,130},{1... | collective-permute-start | bytes 49160 | tf_op jit(solution)/shard_map/ppermute | solution.py:14
  305.8 2.8 collective-permute-start.5
  308.7 10.5 %collective-permute-start.8 = (bf16[1,4,4,512]{3,2,1,0:T(4,128)(2,1)S(1)}, bf16[1,4,4,512]{3,2,1,0:T(4,128)(2,1)S(1)}, u32[]{:S(2)}, u32[]{:S(2)}) collective-permute-start(bf16[1,4,4,512]{3,2,1,0:T(4,128)(2,1)S(1)} %convert_element_type.286), channel_id=1, source_target_pairs={{0,128},{128,256},{256,384},{1,129},{129,257},{257,385},{2,130},{1... | collective-permute-start | bytes 49160 | tf_op jit(solution)/shard_map/ppermute | solution.py:14
  317.2 2.8 collective-permute-start.7
  320.2 10.5 %collective-permute-start.10 = (bf16[1,4,4,512]{3,2,1,0:T(4,128)(2,1)S(1)}, bf16[1,4,4,512]{3,2,1,0:T(4,128)(2,1)S(1)}, u32[]{:S(2)}, u32[]{:S(2)}) collective-permute-start(bf16[1,4,4,512]{3,2,1,0:T(4,128)(2,1)S(1)} %convert_element_type.291), channel_id=1, source_target_pairs={{0,128},{128,256},{256,384},{1,129},{129,257},{257,385},{2,130},{1... | collective-permute-start | bytes 49160 | tf_op jit(solution)/shard_map/ppermute | solution.py:14
  323.9 7.6 %collective-permute-start.9 = (bf16[1,4,4,512]{3,2,1,0:T(4,128)(2,1)S(1)}, bf16[1,4,4,512]{3,2,1,0:T(4,128)(2,1)S(1)}, u32[]{:S(2)}, u32[]{:S(2)}) collective-permute-start(bf16[1,4,4,512]{3,2,1,0:T(4,128)(2,1)S(1)} %convert_element_type.289), channel_id=1, source_target_pairs={{0,128},{128,256},{256,384},{1,129},{129,257},{257,385},{2,130},{1... | collective-permute-start | bytes 49160 | tf_op jit(solution)/shard_map/ppermute | solution.py:14
  331.7 6.0 %collective-permute-start.11 = (bf16[1,5,4,4,512]{4,1,3,2,0:T(8,128)(2,1)S(1)}, bf16[1,5,4,4,512]{4,1,3,2,0:T(8,128)(2,1)S(1)}, u32[]{:S(2)}, u32[]{:S(2)}) collective-permute-start(bf16[1,5,4,4,512]{4,1,3,2,0:T(8,128)(2,1)S(1)} %convert_element_type.296), channel_id=1, source_target_pairs={{128,0},{256,128},{384,256},{129,1},{257,129},{385,257},{130,2},{2... | collective-permute-start | bytes 245768 | tf_op jit(solution)/shard_map/ppermute | solution.py:14
  337.8 5.7 %collective-permute-start.12 = (bf16[1,5,4,4,512]{4,1,3,2,0:T(8,128)(2,1)S(1)}, bf16[1,5,4,4,512]{4,1,3,2,0:T(8,128)(2,1)S(1)}, u32[]{:S(2)}, u32[]{:S(2)}) collective-permute-start(bf16[1,5,4,4,512]{4,1,3,2,0:T(8,128)(2,1)S(1)} %convert_element_type.301), channel_id=1, source_target_pairs={{128,0},{256,128},{384,256},{129,1},{257,129},{385,257},{130,2},{2... | collective-permute-start | bytes 245768 | tf_op jit(solution)/shard_map/ppermute | solution.py:14
  343.6 20.4 %collective-permute-start.13 = (bf16[1,5,4,4,512]{4,1,3,2,0:T(8,128)(2,1)S(1)}, bf16[1,5,4,4,512]{4,1,3,2,0:T(8,128)(2,1)S(1)}, u32[]{:S(2)}, u32[]{:S(2)}) collective-permute-start(bf16[1,5,4,4,512]{4,1,3,2,0:T(8,128)(2,1)S(1)} %convert_element_type.306), channel_id=1, source_target_pairs={{128,0},{256,128},{384,256},{129,1},{257,129},{385,257},{130,2},{2... | collective-permute-start | bytes 245768 | tf_op jit(solution)/shard_map/ppermute | solution.py:14
  368.5 6.1 %collective-permute-start.14 = (bf16[1,5,4,4,512]{4,1,3,2,0:T(8,128)(2,1)S(1)}, bf16[1,5,4,4,512]{4,1,3,2,0:T(8,128)(2,1)S(1)}, u32[]{:S(2)}, u32[]{:S(2)}) collective-permute-start(bf16[1,5,4,4,512]{4,1,3,2,0:T(8,128)(2,1)S(1)} %convert_element_type.311), channel_id=1, source_target_pairs={{128,0},{256,128},{384,256},{129,1},{257,129},{385,257},{130,2},{2... | collective-permute-start | bytes 245768 | tf_op jit(solution)/shard_map/ppermute | solution.py:14
  379.5 14.0 %collective-permute-start.15 = (f32[2,5]{1,0:T(2,128)S(1)}, f32[2,5]{1,0:T(2,128)S(1)}, u32[]{:S(2)}, u32[]{:S(2)}) collective-permute-start(f32[2,5]{1,0:T(2,128)S(1)} %fusion.174), channel_id=1, source_target_pairs={{0,16},{16,0},{32,48},{48,32},{64,80},{80,64},{96,112},{112,96},{1... | collective-permute-start | bytes 128 | tf_op jit(solution)/shard_map/ppermute | solution.py:20
Sparse Core Ops, SparseCore 0:
  29.2 251.3 all-gather.1
